TPU v7x, 256 devices: a whole 4x4x8 slice. The times are simulated.
256 devices in a mesh: case: 4 (over y_hi, core), mod: 64 (over x, y_lo, z).
Axes of the slice: x: 4, y: 4 (y_hi: 2, y_lo: 2; y = y_hi * 2 + y_lo), z: 8, core: 2. Of those that a mesh axis runs over, the one named last changes fastest.
Arguments:
- turbulence: float32 [4, 256, 256], P('case'), may hold values from -6 to 6
- pupil_amp: float32 [256, 256], replicated, may hold values from 0.3 to 1
- mod_points: int32 [64], P('mod'), may hold values from 0 to 255
- valid_pix: int32 [65536], P('mod'), may hold values from 0 to 262143, as said below
- recon: bfloat16 [5120, 65536], P('case', 'mod'), may hold values from -0.0234375 to 0.0234375
- gx: float32 [256, 64], replicated, may hold values from -1.2 to 1.2
- gy: float32 [256, 80], replicated, may hold values from -1.2 to 1.2
- act_map: int32 [5120], replicated, may hold values from 0 to 5119, each once
Outputs:
- command_total: float32 [4, 5120], P('case')
- frame: float32 [4, 512, 512], P('case', 'mod')
Inputs may be any that keep to these rules, and one draw needn't show every extreme that they name: `valid_pix`: entries k * 1024 to (k + 1) * 1024 - 1 are flat indices (row times 512 plus column) of pixels in detector rows k * 8 to (k + 1) * 8 - 1.
All inputs are finite; a program needn't handle non-finite values.
Results may differ from a plain program's by a relative error of at most 0.0058.
Values may be sent and summed in bfloat16 or wider, within the bound.
A program may use at most 64 MiB of HBM per device.

v0:
```python
import math
import jax
import jax.numpy as jnp
from jax import lax
from jax.sharding import PartitionSpec as P

STEPS = 2
loop_gain = 0.5
radius_pixels = 6.0
point_count = 256


def phase_table(length, pupil_width, sign_factor):
    centred = jnp.arange(length, dtype=jnp.int32) - length // 2
    position = jnp.arange(pupil_width, dtype=jnp.int32)
    wrapped = jnp.mod(centred[:, None] * position[None, :], length).astype(jnp.float32)
    angles = 2.0 * math.pi / length * wrapped
    factor = 1.0 / math.sqrt(length)
    return (jnp.cos(angles) * factor, sign_factor * jnp.sin(angles) * factor)


def optics_tables(pupil_size, length):
    fwd_cos, fwd_sin = phase_table(length, pupil_size, -1.0)
    inv_cos, inv_sin = phase_table(length, length, 1.0)
    inv_cos = inv_cos.T
    inv_sin = inv_sin.T
    table_one = jnp.concatenate([fwd_cos, fwd_sin], 0).astype(jnp.bfloat16)
    table_two = jnp.concatenate(
        [jnp.concatenate([fwd_cos.T, fwd_sin.T], 1), jnp.concatenate([-fwd_sin.T, fwd_cos.T], 1)], 0
    ).astype(jnp.bfloat16)
    table_three = jnp.concatenate([inv_cos, inv_sin], 0).astype(jnp.bfloat16)
    table_four = jnp.concatenate(
        [jnp.concatenate([inv_cos.T, inv_sin.T], 1), jnp.concatenate([-inv_sin.T, inv_cos.T], 1)], 0
    ).astype(jnp.bfloat16)
    offset = jnp.abs(jnp.arange(length, dtype=jnp.float32) - length // 2)
    mask_angle = 0.5 * math.pi * (offset[:, None] + offset[None, :])
    return (table_one, table_two, table_three, table_four, jnp.cos(mask_angle), jnp.sin(mask_angle))


def detector_frame(pupil_phase, amplitude, mod_point, tables):
    table_one, table_two, table_three, table_four, mask_cos, mask_sin = tables
    pupil_size = pupil_phase.shape[0]
    length = mask_cos.shape[0]
    centred = jnp.arange(pupil_size, dtype=jnp.float32) - pupil_size // 2
    tilt_angle = 2.0 * math.pi / point_count * mod_point.astype(jnp.float32)
    tilt_phase = (
        2.0
        * math.pi
        * radius_pixels
        / length
        * (centred[:, None] * jnp.cos(tilt_angle) + centred[None, :] * jnp.sin(tilt_angle))
    )
    total_phase = pupil_phase + tilt_phase
    pupil_field = jnp.concatenate(
        [amplitude * jnp.cos(total_phase), amplitude * jnp.sin(total_phase)], 1
    ).astype(jnp.bfloat16)
    section_one = jnp.dot(table_one, pupil_field, preferred_element_type=jnp.float32)
    real_part = section_one[:length, :pupil_size] - section_one[length:, pupil_size:]
    imag_part = section_one[:length, pupil_size:] + section_one[length:, :pupil_size]
    focal_half = jnp.concatenate([real_part, imag_part], 1).astype(jnp.bfloat16)
    focal_field = jnp.dot(focal_half, table_two, preferred_element_type=jnp.float32)
    focal_real = focal_field[:, :length]
    focal_imag = focal_field[:, length:]
    masked = jnp.concatenate(
        [
            focal_real * mask_cos - focal_imag * mask_sin,
            focal_real * mask_sin + focal_imag * mask_cos,
        ],
        1,
    ).astype(jnp.bfloat16)
    section_three = jnp.dot(table_three, masked, preferred_element_type=jnp.float32)
    inverse_half = jnp.concatenate(
        [
            section_three[:length, :length] - section_three[length:, length:],
            section_three[:length, length:] + section_three[length:, :length],
        ],
        1,
    ).astype(jnp.bfloat16)
    detector_field = jnp.dot(inverse_half, table_four, preferred_element_type=jnp.float32)
    return detector_field[:, :length] ** 2 + detector_field[:, length:] ** 2


def mirror_surface(commands, act_map, gx, gy):
    actuator_grid = commands[act_map].reshape(gx.shape[1], gy.shape[1])
    rows_mapped = jnp.dot(
        gx, actuator_grid, precision=lax.Precision.HIGHEST, preferred_element_type=jnp.float32
    )
    return jnp.dot(
        rows_mapped, gy.T, precision=lax.Precision.HIGHEST, preferred_element_type=jnp.float32
    )


def body(turbulence, pupil_amp, mod_points, valid_pix, recon, gx, gy, act_map):
    pupil_size = pupil_amp.shape[0]
    length = 2 * pupil_size
    tables = optics_tables(pupil_size, length)
    screen = turbulence[0]
    mod_point = mod_points[0]
    devices_mod = lax.axis_size("mod")
    row_count = length // devices_mod
    command_total = jnp.zeros((1, act_map.shape[0]), jnp.float32)
    pupil_phase = screen
    frame_block = jnp.zeros((row_count, length), jnp.float32)
    for iteration in range(STEPS):
        frame_term = detector_frame(pupil_phase, pupil_amp, mod_point, tables) / devices_mod
        summed = lax.psum(frame_term, "mod")
        frame_block = lax.dynamic_slice_in_dim(
            summed, lax.axis_index("mod") * row_count, row_count, 0
        )
        local_index = valid_pix - lax.axis_index("mod") * (row_count * length)
        signal = frame_block.reshape(-1)[local_index].astype(jnp.bfloat16)
        signals = lax.all_gather(signal[None, :], "case", axis=0, tiled=True)
        partial_commands = lax.dot_general(
            signals, recon, (((1,), (1,)), ((), ())), preferred_element_type=jnp.float32
        )
        summed_commands = lax.psum(partial_commands, "mod")
        own_commands = lax.all_to_all(
            summed_commands, "case", split_axis=0, concat_axis=1, tiled=True
        )
        command_total = command_total + loop_gain * own_commands
        if iteration + 1 < STEPS:
            pupil_phase = screen - mirror_surface(command_total[0], act_map, gx, gy)
    return (command_total, frame_block[None])


def solution(mesh):
    return jax.shard_map(
        body,
        mesh=mesh,
        in_specs=(P("case", None, None), P(), P("mod"), P("mod"), P("case", "mod"), P(), P(), P()),
        out_specs=(P("case", None), P("case", "mod", None)),
        check_vma=False,
    )
```

profile of v0, /device:TPU:1, one launch (start us, length us, event | category | flops | bytes accessed | tf_op | source)
XLA Modules:
  0.0 1675.0 jit_solution(15463527894372798279)
XLA Ops:
  8.2 3.1 multiply_convert_fusion.5
  11.3 3.1 fusion.64
  14.4 9.8 fusion.39
  26.6 1.5 fusion.66
  29.0 4.7 subtract_convert_fusion.1
  33.7 1.3 fusion.15
  38.9 267.6 %all-reduce.4 = bf16[512,512]{1,0:T(8,128)(2,1)} all-reduce(f32[512,512]{1,0:T(8,128)} %fusion.12), channel_id=1, replica_groups=mesh['case'=4,'mod'=64] {'mod'}, use_global_device_ids=true, to_apply=%region_0.1 | all-reduce | flops 262144 | bytes 1572864 | tf_op jit(solution)/shard_map/psum | solution.py:106
  307.3 6.8 gather_fusion
  314.1 62.2 %all-gather = bf16[4096]{0:T(1024)(128)(2,1)S(1)} all-gather(bf16[1024]{0:T(1024)(128)(2,1)S(1)} %gather_fusion), channel_id=2, replica_groups=mesh['case'=4,'mod'=64] {'case'}, dimensions={0}, use_global_device_ids=true | all-gather | bytes 10240 | tf_op jit(solution)/shard_map/all_gather | solution.py:112
  377.1 247.9 %psum.29 = f32[4,1,1280]{2,0,1:T(4,128)S(1)} all-reduce(f32[4,1,1280]{2,0,1:T(4,128)S(1)} %convolution_bitcast_fusion.1), channel_id=1, replica_groups=mesh['case'=4,'mod'=64] {'mod'}, use_global_device_ids=true, to_apply=%region_1.2 | all-reduce | flops 5120 | bytes 40960 | tf_op jit(solution)/shard_map/psum | solution.py:116
  625.6 59.2 %all-to-all-start = ((f32[4,1,1280]{2,1,0:T(1,128)}), f32[4,1,1280]{2,1,0:T(1,128)S(1)}, u32[]{:S(2)}, u32[]{:S(2)}) async-start(f32[4,1,1280]{2,1,0:T(1,128)} %copy.23), calls=%async_computation | async-start | bytes 40960 | tf_op jit(solution)/shard_map/all_to_all | solution.py:117
  684.8 4.6 all-to-all-done
  689.4 28.7 %gather_fusion.1 = f32[5120]{0:T(1024)S(1)} fusion(f32[5120]{0:T(1024)S(1)} %bitcast.31, s32[5120]{0:T(1024)S(1)} %fusion.73), kind=kCustom, calls=%fused_computation.1 | custom fusion | bytes 61440 | tf_op jit(solution)/shard_map/gather | solution.py:84
  719.3 2.2 multiply_convert_fusion.7
  721.6 1.5 fusion.65
  724.0 4.7 subtract_convert_fusion
  728.7 1.3 fusion.23
  733.9 554.2 %all-reduce.3.cloned.1.call-done = f32[512,512]{1,0:T(8,128)} async-done(((f32[512,512]{1,0:T(8,128)}), f32[512,512]{1,0:T(8,128)}) %all-reduce.3.cloned.1.call-update) | async-done | bytes 1048592 | tf_op jit(solution)/shard_map/psum | solution.py:106
  1288.8 6.8 gather_fusion.2
  1295.6 54.1 %all-gather.1 = bf16[4096]{0:T(1024)(128)(2,1)S(1)} all-gather(bf16[1024]{0:T(1024)(128)(2,1)S(1)} %gather_fusion.2), channel_id=3, replica_groups=mesh['case'=4,'mod'=64] {'case'}, dimensions={0}, use_global_device_ids=true | all-gather | bytes 10240 | tf_op jit(solution)/shard_map/all_gather | solution.py:112
  1350.5 252.5 %psum.31 = f32[4,1,1280]{2,0,1:T(4,128)S(1)} all-reduce(f32[4,1,1280]{2,0,1:T(4,128)S(1)} %convolution_bitcast_fusion), channel_id=1, replica_groups=mesh['case'=4,'mod'=64] {'mod'}, use_global_device_ids=true, to_apply=%region_3.4 | all-reduce | flops 5120 | bytes 40960 | tf_op jit(solution)/shard_map/psum | solution.py:116
  1603.7 59.3 %all-to-all-start.1 = ((f32[4,1,1280]{2,1,0:T(1,128)}), f32[4,1,1280]{2,1,0:T(1,128)S(1)}, u32[]{:S(2)}, u32[]{:S(2)}) async-start(f32[4,1,1280]{2,1,0:T(1,128)} %copy.26), calls=%async_computation.1 | async-start | bytes 40960 | tf_op jit(solution)/shard_map/all_to_all | solution.py:117
  1662.9 1.3 dynamic-slice_bitcast_fusion.1
  1664.2 3.3 all-to-all-done.1
  (74 shorter events, 18.0 us)
Async XLA Ops:
  7.2 369.1 %copy-start = (bf16[1280,1024]{1,0:T(8,128)(2,1)S(1)}, bf16[1280,1024]{1,0:T(8,128)(2,1)}, u32[]{:S(2)}) copy-start(bf16[1280,1024]{1,0:T(8,128)(2,1)} %param.12) | copy-start | bytes 7864324
  7.2 17.0 %copy-start.17 = (f32[1,256,256]{2,1,0:T(8,128)S(1)}, f32[1,256,256]{2,1,0:T(8,128)}, u32[]{:S(2)}) copy-start(f32[1,256,256]{2,1,0:T(8,128)} %param.8) | copy-start | bytes 786436
  26.6 1.7 copy-start.11
  26.6 1.7 copy-start.13
  26.6 1.7 copy-start.15
  29.0 4.7 copy-start.7
  29.0 4.7 copy-start.9
  35.0 1.0 copy-start.1
  35.1 1.2 copy-start.3
  35.1 1.3 copy-start.5
  37.7 269.6 %copy-start.19 = (s32[1024]{0:T(1024)S(1)}, s32[1024]{0:T(1024)}, u32[]{:S(2)}) copy-start(s32[1024]{0:T(1024)} %param.11) | copy-start | bytes 12292
  307.3 377.5 %copy-start.18 = (s32[5120]{0:T(1024)S(1)}, s32[5120]{0:T(1024)}, u32[]{:S(2)}) copy-start(s32[5120]{0:T(1024)} %param.15) | copy-start | bytes 61444
  625.6 63.8 %all-to-all-start = ((f32[4,1,1280]{2,1,0:T(1,128)}), f32[4,1,1280]{2,1,0:T(1,128)S(1)}, u32[]{:S(2)}, u32[]{:S(2)}) async-start(f32[4,1,1280]{2,1,0:T(1,128)} %copy.23), calls=%async_computation | async-start | bytes 40960 | tf_op jit(solution)/shard_map/all_to_all | solution.py:117
  684.8 603.3 %all-reduce.3.cloned.1.call-start = ((), (), s32[]{:S(2)}) async-start(), calls=%async_computation.2 | async-start | bytes 2097152 | tf_op jit(solution)/shard_map/psum | solution.py:106
  721.5 1.7 copy-start.12
  721.5 1.7 copy-start.14
  721.5 1.7 copy-start.16
  724.0 4.7 copy-start.8
  724.0 4.7 copy-start.10
  730.0 1.0 copy-start.2
  730.0 1.2 copy-start.4
  730.0 1.3 copy-start.6
  1603.7 63.9 %all-to-all-start.1 = ((f32[4,1,1280]{2,1,0:T(1,128)}), f32[4,1,1280]{2,1,0:T(1,128)S(1)}, u32[]{:S(2)}, u32[]{:S(2)}) async-start(f32[4,1,1280]{2,1,0:T(1,128)} %copy.26), calls=%async_computation.1 | async-start | bytes 40960 | tf_op jit(solution)/shard_map/all_to_all | solution.py:117
Sparse Core Ops, SparseCore 0:
  734.0 554.0 all-reduce.2
where the time goes:
time: 1680 us
  blocking collectives  884 us (53%)
  waiting for transfers between devices  562 us (33%)
  starting transfers between devices  118 us (7%)
  local copies, waits for them, and re-layouts  49.6 us (3%)
  other arithmetic  30.7 us (2%)
    psum x1, waiting for transfers between devices, body(): summed = lax.psum(frame_term, 'mod')  554 us
    psum x2, blocking collectives, body(): summed_commands = lax.psum(partial_commands, 'mod')  500 us
    psum x1, blocking collectives, body(): summed = lax.psum(frame_term, 'mod')  268 us
    all_to_all x2, starting transfers between devices, body(): lax.all_to_all(summed_commands, 'case', split_axis=0, concat_axis=1, tile...  118 us
    all_gather x2, blocking collectives, body(): signals = lax.all_gather(signal[None, :], 'case', axis=0, tiled=True)  116 us
  transfers between devices with their start and end apart: 3, of which 3 were waited for; matrix products, arithmetic and copies ran while one was open for 0% of the time, Pallas kernels for 0%

commit v1 on v0

--- a/solution.py
+++ b/solution.py
@@ -109,7 +109,10 @@
         )
         local_index = valid_pix - lax.axis_index("mod") * (row_count * length)
         signal = frame_block.reshape(-1)[local_index].astype(jnp.bfloat16)
-        signals = lax.all_gather(signal[None, :], "case", axis=0, tiled=True)
+        signals = jnp.concatenate(
+            lax.all_to_all(jnp.stack([signal[None, :]] * lax.axis_size("case")), "case", 0, 0),
+            axis=0,
+        )
         partial_commands = lax.dot_general(
             signals, recon, (((1,), (1,)), ((), ())), preferred_element_type=jnp.float32
         )

time: 1680 us -> 1680 us (level)
    all_to_all x0 -> x2, blocking collectives: none -> 120 us  [body(): lax.all_to_all(jnp.stack([signal[None, :]] * lax.axis_size('case')), 'cas...]
    all_gather x2 -> x0, blocking collectives: 116 us -> none  [body(): signals = lax.all_gather(signal[None, :], 'case', axis=0, tiled=True)]
where the time goes in v1:
time: 1680 us
  blocking collectives  887 us (53%)
  waiting for transfers between devices  562 us (33%)
  starting transfers between devices  118 us (7%)
  local copies, waits for them, and re-layouts  50.1 us (3%)
  other arithmetic  32.1 us (2%)
    psum x1, waiting for transfers between devices, body(): summed = lax.psum(frame_term, 'mod')  554 us
    psum x2, blocking collectives, body(): summed_commands = lax.psum(partial_commands, 'mod')  499 us
    psum x1, blocking collectives, body(): summed = lax.psum(frame_term, 'mod')  268 us
    all_to_all x2, blocking collectives, body(): lax.all_to_all(jnp.stack([signal[None, :]] * lax.axis_size('case')), 'cas...  120 us
    all_to_all x2, starting transfers between devices, body(): lax.all_to_all(summed_commands, 'case', split_axis=0, concat_axis=1, tile...  118 us
  transfers between devices with their start and end apart: 3, of which 3 were waited for; matrix products, arithmetic and copies ran while one was open for 0% of the time, Pallas kernels for 0%

profile of v1, /device:TPU:1, one launch (start us, length us, event | category | flops | bytes accessed | tf_op | source)
XLA Modules:
  0.0 1679.7 jit_solution(286724778800035173)
XLA Ops:
  8.2 3.2 multiply_convert_fusion.5
  11.3 3.1 fusion.64
  14.4 9.8 fusion.39
  26.6 1.5 fusion.66
  29.0 4.7 subtract_convert_fusion.1
  33.7 1.3 fusion.15
  38.9 267.6 %all-reduce.4 = bf16[512,512]{1,0:T(8,128)(2,1)} all-reduce(f32[512,512]{1,0:T(8,128)} %fusion.12), channel_id=1, replica_groups=mesh['case'=4,'mod'=64] {'mod'}, use_global_device_ids=true, to_apply=%region_0.1 | all-reduce | flops 262144 | bytes 1572864 | tf_op jit(solution)/shard_map/psum | solution.py:106
  307.3 6.8 gather_fusion
  315.3 64.2 %all_to_all.36 = bf16[4,2,512]{2,1,0:T(2,128)(2,1)S(1)} all-to-all(bf16[4,2,512]{2,1,0:T(2,128)(2,1)S(1)} %reshape.138), channel_id=1, replica_groups=mesh['case'=4,'mod'=64] {'case'}, dimensions={0} | all-to-all | bytes 16384 | tf_op jit(solution)/shard_map/all_to_all | solution.py:113
  380.4 247.6 %psum.29 = f32[4,1,1280]{2,0,1:T(4,128)S(1)} all-reduce(f32[4,1,1280]{2,0,1:T(4,128)S(1)} %convolution_bitcast_fusion.1), channel_id=1, replica_groups=mesh['case'=4,'mod'=64] {'mod'}, use_global_device_ids=true, to_apply=%region_1.2 | all-reduce | flops 5120 | bytes 40960 | tf_op jit(solution)/shard_map/psum | solution.py:119
  628.5 59.1 %all-to-all-start.1 = ((f32[4,1,1280]{2,1,0:T(1,128)}), f32[4,1,1280]{2,1,0:T(1,128)S(1)}, u32[]{:S(2)}, u32[]{:S(2)}) async-start(f32[4,1,1280]{2,1,0:T(1,128)} %copy.23), calls=%async_computation.1 | async-start | bytes 40960 | tf_op jit(solution)/shard_map/all_to_all | solution.py:120
  687.7 4.6 all-to-all-done.1
  692.3 28.7 %gather_fusion.1 = f32[5120]{0:T(1024)S(1)} fusion(f32[5120]{0:T(1024)S(1)} %bitcast.35, s32[5120]{0:T(1024)S(1)} %fusion.73), kind=kCustom, calls=%fused_computation.1 | custom fusion | bytes 61440 | tf_op jit(solution)/shard_map/gather | solution.py:84
  722.2 2.2 multiply_convert_fusion.7
  724.4 1.5 fusion.65
  726.9 4.7 subtract_convert_fusion
  731.6 1.3 fusion.23
  736.8 554.2 %all-reduce.3.cloned.1.call-done = f32[512,512]{1,0:T(8,128)} async-done(((f32[512,512]{1,0:T(8,128)}), f32[512,512]{1,0:T(8,128)}) %all-reduce.3.cloned.1.call-update) | async-done | bytes 1048592 | tf_op jit(solution)/shard_map/psum | solution.py:106
  1291.7 6.8 gather_fusion.2
  1299.3 56.0 %all_to_all.37 = bf16[4,2,512]{2,1,0:T(2,128)(2,1)S(1)} all-to-all(bf16[4,2,512]{2,1,0:T(2,128)(2,1)S(1)} %reshape.140), channel_id=1, replica_groups=mesh['case'=4,'mod'=64] {'case'}, dimensions={0} | all-to-all | bytes 16384 | tf_op jit(solution)/shard_map/all_to_all | solution.py:113
  1356.0 251.6 %psum.31 = f32[4,1,1280]{2,0,1:T(4,128)S(1)} all-reduce(f32[4,1,1280]{2,0,1:T(4,128)S(1)} %convolution_bitcast_fusion), channel_id=1, replica_groups=mesh['case'=4,'mod'=64] {'mod'}, use_global_device_ids=true, to_apply=%region_3.4 | all-reduce | flops 5120 | bytes 40960 | tf_op jit(solution)/shard_map/psum | solution.py:119
  1608.2 59.4 %all-to-all-start.3 = ((f32[4,1,1280]{2,1,0:T(1,128)}), f32[4,1,1280]{2,1,0:T(1,128)S(1)}, u32[]{:S(2)}, u32[]{:S(2)}) async-start(f32[4,1,1280]{2,1,0:T(1,128)} %copy.26), calls=%async_computation.3 | async-start | bytes 40960 | tf_op jit(solution)/shard_map/all_to_all | solution.py:120
  1667.6 1.3 dynamic-slice_bitcast_fusion.1
  1668.9 3.3 all-to-all-done.3
  (81 shorter events, 20.0 us)
Async XLA Ops:
  7.2 372.4 %copy-start = (bf16[1280,1024]{1,0:T(8,128)(2,1)S(1)}, bf16[1280,1024]{1,0:T(8,128)(2,1)}, u32[]{:S(2)}) copy-start(bf16[1280,1024]{1,0:T(8,128)(2,1)} %param.12) | copy-start | bytes 7864324
  7.2 17.0 %copy-start.17 = (f32[1,256,256]{2,1,0:T(8,128)S(1)}, f32[1,256,256]{2,1,0:T(8,128)}, u32[]{:S(2)}) copy-start(f32[1,256,256]{2,1,0:T(8,128)} %param.8) | copy-start | bytes 786436
  26.6 1.7 copy-start.11
  26.6 1.7 copy-start.13
  26.6 1.7 copy-start.15
  29.0 4.7 copy-start.7
  29.0 4.7 copy-start.9
  35.0 1.0 copy-start.1
  35.1 1.2 copy-start.3
  35.1 1.3 copy-start.5
  37.7 269.6 %copy-start.19 = (s32[1024]{0:T(1024)S(1)}, s32[1024]{0:T(1024)}, u32[]{:S(2)}) copy-start(s32[1024]{0:T(1024)} %param.11) | copy-start | bytes 12292
  307.3 380.4 %copy-start.18 = (s32[5120]{0:T(1024)S(1)}, s32[5120]{0:T(1024)}, u32[]{:S(2)}) copy-start(s32[5120]{0:T(1024)} %param.15) | copy-start | bytes 61444
  628.5 63.8 %all-to-all-start.1 = ((f32[4,1,1280]{2,1,0:T(1,128)}), f32[4,1,1280]{2,1,0:T(1,128)S(1)}, u32[]{:S(2)}, u32[]{:S(2)}) async-start(f32[4,1,1280]{2,1,0:T(1,128)} %copy.23), calls=%async_computation.1 | async-start | bytes 40960 | tf_op jit(solution)/shard_map/all_to_all | solution.py:120
  687.6 603.3 %all-reduce.3.cloned.1.call-start = ((), (), s32[]{:S(2)}) async-start(), calls=%async_computation.4 | async-start | bytes 2097152 | tf_op jit(solution)/shard_map/psum | solution.py:106
  724.4 1.7 copy-start.12
  724.4 1.7 copy-start.14
  724.4 1.7 copy-start.16
  726.9 4.7 copy-start.8
  726.9 4.7 copy-start.10
  732.9 1.0 copy-start.2
  732.9 1.2 copy-start.4
  732.9 1.3 copy-start.6
  1608.2 64.0 %all-to-all-start.3 = ((f32[4,1,1280]{2,1,0:T(1,128)}), f32[4,1,1280]{2,1,0:T(1,128)S(1)}, u32[]{:S(2)}, u32[]{:S(2)}) async-start(f32[4,1,1280]{2,1,0:T(1,128)} %copy.26), calls=%async_computation.3 | async-start | bytes 40960 | tf_op jit(solution)/shard_map/all_to_all | solution.py:120
Sparse Core Ops, SparseCore 0:
  736.9 554.0 all-reduce.2
